TPU v7x, 512 devices: a whole 4x4x16 slice. The times are simulated.
512 devices in a mesh: dp: 64 (over z, x), feat: 8 (over y, core).
Axes of the slice: x: 4, y: 4, z: 16, core: 2. Of those that a mesh axis runs over, the one named last changes fastest.
Arguments:
- grads: bfloat16 [8, 32768, 4, 128], P('feat', 'dp'), may hold values from -6 to 6
- block_ids: int32 [8, 32768, 4], P('feat', 'dp'), may hold values from 0 to 127, all different within a row; in each aligned block of 512 rows (0 to 511, 512 to 1023, ..., all dimensions but the last counted through in order) at most 24 rows name the same one
- probe: bfloat16 [128, 8, 128, 512], P('dp', 'feat'), may hold values from -0.09375 to 0.09375
Outputs:
- whitened: float32 [32768, 512], P(('dp', 'feat'))
Inputs may be any that keep to these rules, and one draw needn't show every extreme that they name: block_ids[j, s, k] is a local block number in slice j; the ids of one sample in one slice are distinct; among the 512 samples of one index of dp, no number appears more than 24 times in one slice, and some number appears exactly 24 times.
All inputs are finite; a program needn't handle non-finite values.
Results may differ from a plain program's by a relative error of at most 0.012.
Values may be sent and summed in bfloat16 or wider, within the bound.
A program may use at most 64 MiB of HBM per device.

v0:
```python
import math

import jax
import jax.numpy as jnp
from jax import lax
from jax.sharding import PartitionSpec as P

ridge = 0.1
root_steps = 4


def shifted(value, axis, steps):
    count = lax.axis_size(axis)
    pairs = [(source, (source + steps) % count) for source in range(count)]
    return lax.ppermute(value, axis, pairs)


def gram_of(rows):
    return lax.dot_general(rows, rows, (((0,), (0,)), ((), ())), preferred_element_type=jnp.float32)


def inverse_root(gram):
    width = gram.shape[0]
    ident = jnp.eye(width, dtype=jnp.float32)
    scale = jnp.trace(gram) / width
    current = gram / scale
    result = ident
    for step in range(root_steps):
        middle = 1.5 * ident - 0.5 * jnp.dot(result, current, precision=lax.Precision.HIGHEST)
        if step + 1 < root_steps:
            current = jnp.dot(current, middle, precision=lax.Precision.HIGHEST)
        result = jnp.dot(middle, result, precision=lax.Precision.HIGHEST)
    return result / jnp.sqrt(scale)


def local(grads, block_ids, probe):
    values = grads[0]
    ids = block_ids[0]
    s_dev, k_j, b_width = values.shape
    n_dp = lax.axis_size("dp")
    n_feat = lax.axis_size("feat")
    per_dev = probe.shape[0]
    width = probe.shape[3]
    b_slice = per_dev * n_dp
    bound = max(2, 3 * s_dev * k_j // (2 * b_slice))
    slots = per_dev * bound
    flat_ids = ids.reshape(-1)
    target = flat_ids // per_dev
    within = flat_ids % per_dev
    onehot = (target[:, None] == jnp.arange(n_dp, dtype=jnp.int32)[None, :]).astype(jnp.int32)
    rank_in = jnp.sum((jnp.cumsum(onehot, axis=0) - onehot) * onehot, axis=1)
    position = target * slots + rank_in
    send_tiles = (
        jnp.zeros((n_dp * slots, b_width), jnp.bfloat16)
        .at[position]
        .set(values.reshape(-1, b_width))
    )
    send_which = jnp.full((n_dp * slots,), per_dev, jnp.int32).at[position].set(within)
    send_tiles = send_tiles.reshape(n_dp, slots, b_width)
    send_which = send_which.reshape(n_dp, slots)
    local_probe = probe[:, 0].reshape(per_dev * b_width, width)
    tiles = lax.all_to_all(send_tiles, "dp", split_axis=0, concat_axis=0, tiled=True)
    which = lax.all_to_all(send_which, "dp", split_axis=0, concat_axis=0, tiled=True)
    pick = (which[..., None] == jnp.arange(per_dev, dtype=jnp.int32)).astype(jnp.bfloat16)
    spread = (pick[..., None] * tiles[..., None, :]).reshape(
        tiles.shape[0], tiles.shape[1], per_dev * b_width
    )
    product = jnp.einsum("ncf,fr->ncr", spread, local_probe, preferred_element_type=jnp.float32)
    returned = lax.all_to_all(
        product.astype(jnp.bfloat16), "dp", split_axis=0, concat_axis=0, tiled=True
    )
    per_tile = returned.reshape(n_dp * slots, width)[position]
    partial_value = jnp.sum(per_tile.reshape(s_dev, k_j, width).astype(jnp.float32), axis=1)
    own_rows = s_dev // n_feat
    summed = lax.psum(partial_value, "feat")
    sketch = summed.astype(jnp.bfloat16)
    gram = gram_of(sketch)
    mine = lax.dynamic_slice_in_dim(sketch, lax.axis_index("feat") * own_rows, own_rows, 0)
    gram = gram + ridge * s_dev * jnp.eye(width, dtype=jnp.float32)
    levels = n_dp.bit_length() - 1
    total = gram
    for level in range(levels):
        total = total + shifted(total, "dp", -(1 << level))
    root = inverse_root(total)
    samples = s_dev * n_dp
    return math.sqrt(samples) * jnp.dot(
        mine.astype(jnp.float32), root, precision=lax.Precision.HIGHEST
    )


def solution(mesh):
    return jax.shard_map(
        local,
        mesh=mesh,
        in_specs=(P("feat", "dp", None, None), P("feat", "dp", None), P("dp", "feat", None, None)),
        out_specs=P(("dp", "feat"), None),
        check_vma=False,
    )
```

profile of v0, /device:TPU:23, one launch (start us, length us, event | category | flops | bytes accessed | tf_op | source)
XLA Modules:
  0.0 687.0 jit_solution(11042305152612590406)
XLA Ops:
  0.0 0.0 copy-start
  0.0 0.9 copy.9
  0.9 0.2 reshape_squeeze.15
  1.1 0.2 reshape_squeeze.14
  1.2 0.2 reshape_squeeze.13
  1.5 18.1 %reduce-window.6 = s32[64,16,128]{2,1,0:T(8,128)S(1)} reduce-window(s32[64,16,128]{2,1,0:T(8,128)S(1)} %fusion.5, s32[]{:T(128)} %constant.52.clone.1), window={size=1x1x128 pad=0_0x0_0x127_0}, to_apply=%region_0.1 | reduce-window | flops 16646144 | bytes 1048580 | tf_op jit(solution)/shard_map/reduce-window
  19.6 0.2 slice.10
  19.8 0.4 copy.15
  20.2 0.2 reduce-window.9
  20.4 0.2 broadcast_add_fusion
  20.7 0.3 fusion.4
  20.9 0.1 compare_select_fusion
  21.0 8.1 %scatter_custom_fusion = s32[3072]{0:T(1024)S(1)} fusion(s32[2048]{0:T(1024)S(1)} %bitcast.60, s32[2048]{0:T(1024)S(1)} %get-tuple-element.7, s32[]{:T(128)} %constant.50.clone.1), kind=kCustom, calls=%fused_computation.53 | custom fusion | bytes 12292 | tf_op jit(solution)/shard_map/scatter | solution.py:58
  29.1 0.7 all_to_all.12
  29.7 18.0 %all-to-all-start = ((s32[64,1,48]{2,1,0:T(1,128)}), s32[64,1,48]{2,1,0:T(1,128)S(1)}, u32[]{:S(2)}, u32[]{:S(2)}) async-start(s32[64,1,48]{2,1,0:T(1,128)} %bitcast.5), calls=%async_computation | async-start | bytes 65536 | tf_op jit(solution)/shard_map/all_to_all | solution.py:63
  47.8 7.0 %scatter_custom_fusion.1 = bf16[3072,128]{1,0:T(8,128)(2,1)} fusion(s32[2048]{0:T(1024)S(1)} %bitcast.61, bf16[2048,128]{1,0:T(8,128)(2,1)} %bitcast.63, bf16[]{:T(256)} %constant.56.clone.1), kind=kCustom, calls=%fused_computation.30 | custom fusion | bytes 786944 | tf_op jit(solution)/shard_map/scatter | solution.py:56
  54.8 4.8 all-to-all-done
  59.5 9.8 %all-to-all-start.1 = ((bf16[64,48,128]{2,1,0:T(8,128)(2,1)}), bf16[64,48,128]{2,1,0:T(8,128)(2,1)S(1)}, u32[]{:S(2)}, u32[]{:S(2)}) async-start(bf16[64,48,128]{2,1,0:T(8,128)(2,1)} %bitcast.8), calls=%async_computation.1 | async-start | bytes 1572864 | tf_op jit(solution)/shard_map/all_to_all | solution.py:62
  69.3 0.6 fusion
  69.9 42.0 %all-to-all-done.1 = bf16[64,48,128]{2,1,0:T(8,128)(2,1)S(1)} async-done(((bf16[64,48,128]{2,1,0:T(8,128)(2,1)}), bf16[64,48,128]{2,1,0:T(8,128)(2,1)S(1)}, u32[]{:S(2)}, u32[]{:S(2)}) %all-to-all-start.1) | async-done | bytes 786464 | tf_op jit(solution)/shard_map/all_to_all | solution.py:62
  111.9 3.8 broadcast_multiply_fusion
  115.7 1.1 mul.84
  116.8 0.0 copy-done
  116.8 2.6 convolution_convert_fusion
  119.4 6.1 all-to-all-start.2
  125.6 141.6 %all-to-all-done.2 = bf16[64,48,512]{2,1,0:T(8,128)(2,1)S(1)} async-done(((bf16[64,48,512]{2,1,0:T(8,128)(2,1)}), bf16[64,48,512]{2,1,0:T(8,128)(2,1)S(1)}, u32[]{:S(2)}, u32[]{:S(2)}) %all-to-all-start.2) | async-done | bytes 3145760 | tf_op jit(solution)/shard_map/all_to_all | solution.py:69
  267.2 9.2 %gather_fusion = bf16[2048,512]{1,0:T(8,128)(2,1)} fusion(bf16[3072,512]{1,0:T(8,128)(2,1)S(1)} %bitcast.54, s32[2048]{0:T(1024)S(1)} %broadcast_clamp_fusion), kind=kCustom, calls=%fused_computation | custom fusion | bytes 4202496 | tf_op jit(solution)/shard_map/gather | solution.py:72
  276.4 4.8 reshape.154
  281.1 4.7 reduce_sum.32
  285.8 51.1 %all-reduce.1 = bf16[512,512]{1,0:T(8,128)(2,1)S(1)} all-reduce(f32[512,512]{1,0:T(8,128)S(1)} %reduce_sum.32), channel_id=1, replica_groups=mesh['dp'=64,'feat'=8] {'feat'}, use_global_device_ids=true, to_apply=%region_6.7 | all-reduce | flops 262144 | bytes 1572864 | tf_op jit(solution)/shard_map/psum | solution.py:75
  336.9 0.0 copy-start.1
  336.9 0.5 convolution_add_fusion
  337.4 3.5 collective-permute-start
  340.9 22.4 %collective-permute-done = f32[512,512]{1,0:T(8,128)S(1)} collective-permute-done((f32[512,512]{1,0:T(8,128)S(1)}, f32[512,512]{1,0:T(8,128)S(1)}, u32[]{:S(2)}, u32[]{:S(2)}) %collective-permute-start) | collective-permute-done | bytes 1048608 | tf_op jit(solution)/shard_map/ppermute | solution.py:15
  363.3 0.2 add.71
  363.5 0.0 copy-done.1
  363.5 2.0 collective-permute-start.1
  365.5 25.3 %collective-permute-done.1 = f32[512,512]{1,0:T(8,128)S(1)} collective-permute-done((f32[512,512]{1,0:T(8,128)S(1)}, f32[512,512]{1,0:T(8,128)S(1)}, u32[]{:S(2)}, u32[]{:S(2)}) %collective-permute-start.1) | collective-permute-done | bytes 1048608 | tf_op jit(solution)/shard_map/ppermute | solution.py:15
  390.8 0.2 add.72
  391.0 2.7 collective-permute-start.2
  393.8 23.3 %collective-permute-done.2 = f32[512,512]{1,0:T(8,128)S(1)} collective-permute-done((f32[512,512]{1,0:T(8,128)S(1)}, f32[512,512]{1,0:T(8,128)S(1)}, u32[]{:S(2)}, u32[]{:S(2)}) %collective-permute-start.2) | collective-permute-done | bytes 1048608 | tf_op jit(solution)/shard_map/ppermute | solution.py:15
  417.0 0.2 add.73
  417.2 3.2 collective-permute-start.3
  420.4 29.5 %collective-permute-done.3 = f32[512,512]{1,0:T(8,128)S(1)} collective-permute-done((f32[512,512]{1,0:T(8,128)S(1)}, f32[512,512]{1,0:T(8,128)S(1)}, u32[]{:S(2)}, u32[]{:S(2)}) %collective-permute-start.3) | collective-permute-done | bytes 1048608 | tf_op jit(solution)/shard_map/ppermute | solution.py:15
  449.9 0.2 add.74
  450.1 6.6 collective-permute-start.4
  456.7 107.1 %collective-permute-done.4 = f32[512,512]{1,0:T(8,128)S(1)} collective-permute-done((f32[512,512]{1,0:T(8,128)S(1)}, f32[512,512]{1,0:T(8,128)S(1)}, u32[]{:S(2)}, u32[]{:S(2)}) %collective-permute-start.4) | collective-permute-done | bytes 1048608 | tf_op jit(solution)/shard_map/ppermute | solution.py:15
  563.8 0.2 add.75
  564.0 6.7 collective-permute-start.5
  570.7 93.6 %collective-permute-done.5 = f32[512,512]{1,0:T(8,128)S(1)} collective-permute-done((f32[512,512]{1,0:T(8,128)S(1)}, f32[512,512]{1,0:T(8,128)S(1)}, u32[]{:S(2)}, u32[]{:S(2)}) %collective-permute-start.5) | collective-permute-done | bytes 1048608 | tf_op jit(solution)/shard_map/ppermute | solution.py:15
  664.3 0.8 select_reduce_fusion
  665.8 1.1 select_subtract_fusion.3
  666.9 1.9 fusion.6
  668.8 1.0 fusion.1
  669.8 1.9 select_subtract_fusion.2
  671.6 1.8 fusion.18
  673.5 1.8 fusion.17
  675.4 1.9 select_subtract_fusion.1
  677.2 2.1 fusion.20
  679.3 1.8 fusion.19
  681.2 1.9 select_subtract_fusion
  683.1 1.8 convolution_divide_fusion
  685.0 2.0 convolution_multiply_fusion.4
  (4 shorter events, 0.1 us)
Async XLA Ops:
  0.0 116.8 %copy-start = (bf16[2,1,128,512]{3,2,1,0:T(8,128)(2,1)S(1)}, bf16[2,1,128,512]{3,2,1,0:T(8,128)(2,1)}, u32[]{:S(2)}) copy-start(bf16[2,1,128,512]{3,2,1,0:T(8,128)(2,1)} %param.5) | copy-start | bytes 786436
  29.7 29.8 %all-to-all-start = ((s32[64,1,48]{2,1,0:T(1,128)}), s32[64,1,48]{2,1,0:T(1,128)S(1)}, u32[]{:S(2)}, u32[]{:S(2)}) async-start(s32[64,1,48]{2,1,0:T(1,128)} %bitcast.5), calls=%async_computation | async-start | bytes 65536 | tf_op jit(solution)/shard_map/all_to_all | solution.py:63
  59.5 52.3 %all-to-all-start.1 = ((bf16[64,48,128]{2,1,0:T(8,128)(2,1)}), bf16[64,48,128]{2,1,0:T(8,128)(2,1)S(1)}, u32[]{:S(2)}, u32[]{:S(2)}) async-start(bf16[64,48,128]{2,1,0:T(8,128)(2,1)} %bitcast.8), calls=%async_computation.1 | async-start | bytes 1572864 | tf_op jit(solution)/shard_map/all_to_all | solution.py:62
  119.4 147.8 %all-to-all-start.2 = ((bf16[64,48,512]{2,1,0:T(8,128)(2,1)}), bf16[64,48,512]{2,1,0:T(8,128)(2,1)S(1)}, u32[]{:S(2)}, u32[]{:S(2)}) async-start(bf16[64,48,512]{2,1,0:T(8,128)(2,1)} %convolution_convert_fusion), calls=%async_computation.2 | async-start | bytes 6291456 | tf_op jit(solution)/shard_map/all_to_all | solution.py:69
  336.9 26.6 %copy-start.1 = (bf16[512,512]{1,0:T(8,128)(2,1)}, bf16[512,512]{1,0:T(8,128)(2,1)S(1)}, u32[]{:S(2)}) copy-start(bf16[512,512]{1,0:T(8,128)(2,1)S(1)} %all-reduce.1) | copy-start | bytes 1572868
  337.4 25.9 %collective-permute-start = (f32[512,512]{1,0:T(8,128)S(1)}, f32[512,512]{1,0:T(8,128)S(1)}, u32[]{:S(2)}, u32[]{:S(2)}) collective-permute-start(f32[512,512]{1,0:T(8,128)S(1)} %convolution_add_fusion), channel_id=1, source_target_pairs={{0,504},{8,0},{16,8},{24,16},{32,24},{40,32},{48,40},{56,48},{64,5... | collective-permute-start | bytes 3145736 | tf_op jit(solution)/shard_map/ppermute | solution.py:15
  363.5 27.3 %collective-permute-start.1 = (f32[512,512]{1,0:T(8,128)S(1)}, f32[512,512]{1,0:T(8,128)S(1)}, u32[]{:S(2)}, u32[]{:S(2)}) collective-permute-start(f32[512,512]{1,0:T(8,128)S(1)} %add.71), channel_id=1, source_target_pairs={{0,496},{8,504},{16,0},{24,8},{32,16},{40,24},{48,32},{56,40},{64,... | collective-permute-start | bytes 3145736 | tf_op jit(solution)/shard_map/ppermute | solution.py:15
  391.0 26.0 %collective-permute-start.2 = (f32[512,512]{1,0:T(8,128)S(1)}, f32[512,512]{1,0:T(8,128)S(1)}, u32[]{:S(2)}, u32[]{:S(2)}) collective-permute-start(f32[512,512]{1,0:T(8,128)S(1)} %add.72), channel_id=1, source_target_pairs={{0,480},{8,488},{16,496},{24,504},{32,0},{40,8},{48,16},{56,24},{6... | collective-permute-start | bytes 3145736 | tf_op jit(solution)/shard_map/ppermute | solution.py:15
  417.2 32.7 %collective-permute-start.3 = (f32[512,512]{1,0:T(8,128)S(1)}, f32[512,512]{1,0:T(8,128)S(1)}, u32[]{:S(2)}, u32[]{:S(2)}) collective-permute-start(f32[512,512]{1,0:T(8,128)S(1)} %add.73), channel_id=1, source_target_pairs={{0,448},{8,456},{16,464},{24,472},{32,480},{40,488},{48,496},{56,5... | collective-permute-start | bytes 3145736 | tf_op jit(solution)/shard_map/ppermute | solution.py:15
  450.1 113.7 %collective-permute-start.4 = (f32[512,512]{1,0:T(8,128)S(1)}, f32[512,512]{1,0:T(8,128)S(1)}, u32[]{:S(2)}, u32[]{:S(2)}) collective-permute-start(f32[512,512]{1,0:T(8,128)S(1)} %add.74), channel_id=1, source_target_pairs={{0,384},{8,392},{16,400},{24,408},{32,416},{40,424},{48,432},{56,4... | collective-permute-start | bytes 3145736 | tf_op jit(solution)/shard_map/ppermute | solution.py:15
  564.0 100.4 %collective-permute-start.5 = (f32[512,512]{1,0:T(8,128)S(1)}, f32[512,512]{1,0:T(8,128)S(1)}, u32[]{:S(2)}, u32[]{:S(2)}) collective-permute-start(f32[512,512]{1,0:T(8,128)S(1)} %add.75), channel_id=1, source_target_pairs={{0,256},{8,264},{16,272},{24,280},{32,288},{40,296},{48,304},{56,3... | collective-permute-start | bytes 3145736 | tf_op jit(solution)/shard_map/ppermute | solution.py:15
where the time goes:
time: 688 us; the launch traced here: 687 us
  waiting for transfers between devices  489 us (71%)
  starting transfers between devices  58.7 us (9%)
  blocking collectives  51.1 us (7%)
  local copies, waits for them, and re-layouts  32.8 us (5%)
  other arithmetic  29.8 us (4%)
  matrix products  24.2 us (4%)
    ppermute x6, waiting for transfers between devices, shifted(): return lax.ppermute(value, axis, pairs)  301 us
    all_to_all x1, waiting for transfers between devices, local(): lax.all_to_all(product.astype(jnp.bfloat16), 'dp', split_axis=0, concat_a...  142 us
    psum x1, blocking collectives, local(): summed = lax.psum(partial_value, 'feat')  51.1 us
    all_to_all x1, waiting for transfers between devices, local(): lax.all_to_all(send_tiles, 'dp', split_axis=0, concat_axis=0, tiled=True)  42 us
    ppermute x6, starting transfers between devices, shifted(): return lax.ppermute(value, axis, pairs)  24.8 us
    another operation x3, other arithmetic  18.5 us
    all_to_all x1, starting transfers between devices, local(): lax.all_to_all(send_which, 'dp', split_axis=0, concat_axis=0, tiled=True)  18 us
  transfers between devices with their start and end apart: 9, of which 9 were waited for; matrix products, arithmetic and copies ran while one was open for 1% of the time, Pallas kernels for 0%

commit v1 on v0

v1 whole, which is shorter than its diff:
```python
import math

import jax
import jax.numpy as jnp
from jax import lax
from jax.experimental import pallas as pl
from jax.experimental.pallas import tpu as pltpu
from jax.sharding import PartitionSpec as P

ridge = 0.1
root_steps = 4
NX = 4
NC = 2
MESH = pl.DeviceIdType.MESH
bf16, f32 = jnp.bfloat16, jnp.float32


def sizes():
    return lax.axis_size("dp") // NX, lax.axis_size("feat") // NC


class Place:
    def __init__(self, nz, ny):
        dp, feat = lax.axis_index("dp"), lax.axis_index("feat")
        self.nz, self.ny = nz, ny
        self.z, self.x = dp // NX, lax.rem(dp, NX)
        self.y, self.c = feat // NC, lax.rem(feat, NC)

    def at(self, dz=0, dx=0, dy=0, dc=0):
        z = lax.rem(self.z + (dz % self.nz), self.nz)
        x = lax.rem(self.x + (dx % NX), NX)
        y = lax.rem(self.y + (dy % self.ny), self.ny)
        c = lax.rem(self.c + dc, NC)
        return {"dp": z * NX + x, "feat": y * NC + c}


def greet(others):
    barrier = pltpu.get_barrier_semaphore()
    for other in others:
        pl.semaphore_signal(barrier, inc=1, device_id=other, device_id_type=MESH)
    pl.semaphore_wait(barrier, len(others))


def sketch_kernel(
    nz, ny, ge, probe, out,
    gx, codes, dense, pbuf, acc, csend, crecv, xs, xo, xr, rows, ys, yr,
    zss, zrs, xss, xrs, css, crs, oss, ors, qss, qrs, yss, yrs,
):
    here = Place(nz, ny)
    z, x, y, c = here.z, here.x, here.y, here.c
    s_dev, s_ext = 512, ge.shape[0]
    cut = 272
    right_z, left_z = here.at(dz=1), here.at(dz=-1)
    right_x, left_x = here.at(dx=1), here.at(dx=-1)
    other_core = here.at(dc=1)
    greet([right_z, left_z, right_x, left_x, other_core] + [here.at(dy=d) for d in range(1, ny)])

    def remote(src, dst, ssem, rsem, to):
        return pltpu.make_async_remote_copy(
            src_ref=src, dst_ref=dst, send_sem=ssem, recv_sem=rsem, device_id=to, device_id_type=MESH
        )

    half = nz // 2
    started = []

    def go(copy):
        copy.start()
        started.append(copy)

    def zcopy(way, h, s, w):
        src, dst = (s, s + 1) if way == 0 else ((nz - s) % nz, nz - 1 - s)
        part = pl.ds(128 * w, 128)
        return remote(
            pbuf.at[h, src, part], pbuf.at[h, dst, part], zss.at[way, h, s, w], zrs.at[way, h, s, w],
            right_z if way == 0 else left_z,
        )

    def zsent(way, s, w):
        return s < half - 1 or (s == half - 1 and w == way)

    def arrive(h, s):
        for w in range(2):
            for way in range(2):
                if zsent(way, s, w):
                    zcopy(way, h, s, w).wait_recv()
                    if s + 1 < half and zsent(way, s + 1, w):
                        go(zcopy(way, h, s + 1, w))

    def own(h):
        for w in range(2):
            for way in range(2):
                go(zcopy(way, h, 0, w))

    lo, hi = pl.ds(0, cut), pl.ds(cut, s_ext - cut)
    xc = {
        "ra": remote(ge.at[lo], gx.at[0, lo], xss.at[0], xrs.at[0], right_x),
        "rb": remote(ge.at[hi], gx.at[0, hi], xss.at[1], xrs.at[1], right_x),
        "lb": remote(ge.at[hi], gx.at[1, hi], xss.at[2], xrs.at[2], left_x),
        "la": remote(ge.at[lo], gx.at[1, lo], xss.at[3], xrs.at[3], left_x),
        "fa": remote(gx.at[0, lo], gx.at[2, lo], xss.at[4], xrs.at[4], right_x),
        "fb": remote(gx.at[1, hi], gx.at[2, hi], xss.at[5], xrs.at[5], left_x),
    }

    def expand(t):
        src = ge if t == 0 else gx.at[t - 1]
        ids = src[pl.ds(s_dev, 16), :].astype(jnp.int32)
        m = lax.rem(z + nz - ids // 8, nz)
        code = jnp.where(lax.rem(ids // 2, NX) == x, 2 * m + lax.rem(ids, 2), 255).astype(f32).astype(bf16)
        picks = (
            lax.broadcasted_iota(jnp.int32, (16, 512), 0) == lax.broadcasted_iota(jnp.int32, (16, 512), 1) // 128
        ).astype(f32).astype(bf16)
        codes[...] = lax.dot_general(
            code, picks, (((0,), (0,)), ((), ())), preferred_element_type=f32
        ).astype(bf16)

        @pl.loop(0, s_dev // 32)
        def _(i):
            r = pl.ds(pl.multiple_of(i * 32, 32), 32)
            g = [src[r, pl.ds(128 * k, 128)] for k in range(4)]
            q = [codes[r, pl.ds(128 * k, 128)] for k in range(4)]
            for b in range(2 * nz):
                v = jnp.zeros_like(g[0])
                for k in range(4):
                    v = jnp.where(q[k] == jnp.asarray(b, bf16), g[k], v)
                dense[t, r, pl.ds(128 * b, 128)] = v

    def product(h, t, spans, first):
        total = None
        for lo_m, hi_m in spans:
            depth = (hi_m - lo_m) * 256
            term = jnp.dot(
                dense[t, :, pl.ds(lo_m * 256, depth)], pbuf[h, lo_m:hi_m].reshape(depth, 256),
                preferred_element_type=f32,
            )
            total = term if total is None else total + term
        if not first:
            total = total + acc[h, t]
        acc[h, t] = total

    def ccopy(h, t):
        return remote(csend.at[h, t], crecv.at[h, t], css.at[h, t], crs.at[h, t], other_core)

    def give_core(h, t):
        for yy in range(ny):
            csend[h, t, yy] = acc[h, t, pl.ds(pl.multiple_of(128 * yy + 64 * (1 - c), 64), 64), :].astype(bf16)
        go(ccopy(h, t))

    def both(h, t, yy):
        mine = acc[h, t, pl.ds(pl.multiple_of(128 * yy + 64 * c, 64), 64), :]
        return mine + crecv[h, t, yy].astype(f32)

    top, bottom = pl.ds(0, ny // 2), pl.ds(ny // 2, ny // 2)
    tops, bottoms = range(ny // 2), range(ny // 2, ny)

    def ocopy(h, way):
        part = top if way == 0 else bottom
        return remote(
            xs.at[h, 2, part], xo.at[h, way], oss.at[h, way], ors.at[h, way], right_x if way == 0 else left_x
        )

    def qcopy(h, way, part):
        span = top if part == 0 else bottom
        return remote(
            xs.at[h, 1 - way, span], xr.at[h, way, span], qss.at[h, way, part], qrs.at[h, way, part],
            right_x if way == 0 else left_x,
        )

    def ycopy(h, d):
        return remote(ys.at[h, d - 1], yr.at[h, d - 1], yss.at[h, d - 1], yrs.at[h, d - 1], here.at(dy=d))

    def far(h):
        ccopy(h, 3).wait_recv()
        for yy in range(ny):
            xs[h, 2, yy] = both(h, 3, yy).astype(bf16)
        go(ocopy(h, 0))
        go(ocopy(h, 1))

    def near(h):
        ccopy(h, 2).wait_recv()
        for yy in bottoms:
            xs[h, 1, yy] = both(h, 2, yy).astype(bf16)
        go(qcopy(h, 0, 1))
        ccopy(h, 1).wait_recv()
        for yy in tops:
            xs[h, 0, yy] = both(h, 1, yy).astype(bf16)
        go(qcopy(h, 1, 0))

    def joined(h):
        ocopy(h, 0).wait_recv()
        for yy in tops:
            xs[h, 1, yy] = (both(h, 2, yy) + xo[h, 0, yy].astype(f32)).astype(bf16)
        go(qcopy(h, 0, 0))
        ocopy(h, 1).wait_recv()
        for yy in bottoms:
            xs[h, 0, yy] = (both(h, 1, yy) + xo[h, 1, yy - ny // 2].astype(f32)).astype(bf16)
        go(qcopy(h, 1, 1))

    def home(h):
        ccopy(h, 0).wait_recv()
        for way in range(2):
            for part in range(2):
                qcopy(h, way, part).wait_recv()
        for yy in range(ny):
            rows[h, yy] = both(h, 0, yy) + xr[h, 0, yy].astype(f32) + xr[h, 1, yy].astype(f32)
        for d in range(1, ny):
            ys[h, d - 1] = rows[h, lax.rem(y + d, ny)].astype(bf16)
            go(ycopy(h, d))

    def finish(h):
        total = rows[h, y]
        for d in range(1, ny):
            ycopy(h, d).wait_recv()
            total = total + yr[h, d - 1].astype(f32)
        out[:, pl.ds(256 * h, 256)] = total.astype(bf16)

    for h in range(2):
        pbuf[h, 0] = probe[:, pl.ds(256 * h, 256)]
    own(0)
    for name in ("ra", "lb", "rb", "la"):
        go(xc[name])
    expand(0)
    whole = [(0, nz)]
    early, late = [(0, 6), (11, nz)], [(6, 11)]
    for s in range(half):
        arrive(0, s)
        if s == 1:
            xc["ra"].wait_recv()
            go(xc["fa"])
            xc["lb"].wait_recv()
            go(xc["fb"])
        if s == 3:
            xc["rb"].wait_recv()
            expand(1)
        if s == 4:
            xc["la"].wait_recv()
            expand(2)
        if s == half - 2:
            own(1)
    xc["fa"].wait_recv()
    xc["fb"].wait_recv()
    expand(3)
    for s in range(half):
        if s == half - 1:
            product(1, 0, early, True)
        arrive(1, s)
        if s < 4:
            product(0, 3 - s, whole, True)
            give_core(0, 3 - s)
        if s == 2:
            far(0)
        if s == 3:
            near(0)
        if s == 4:
            joined(0)
            home(0)
        if s == 5:
            finish(0)
            product(1, 3, early, True)
        if s == 6:
            product(1, 2, early, True)
            product(1, 1, early, True)
    for t in (3, 2, 1, 0):
        product(1, t, late, False)
        give_core(1, t)
        if t == 2:
            far(1)
        if t == 0:
            near(1)
    joined(1)
    home(1)
    finish(1)
    for copy in started:
        copy.wait_send()


def sketch_rows(grads, block_ids, probe):
    nz, ny = sizes()
    s_dev = grads.shape[1]
    values = grads[0].reshape(s_dev, 512)
    ids = jnp.pad(block_ids[0].T.astype(f32).astype(bf16), ((0, 12), (0, 0)))
    ge = jnp.concatenate([values, ids], axis=0)
    blocks = probe.reshape(256, 512)
    half = nz // 2
    dma = pltpu.SemaphoreType.DMA
    return pl.pallas_call(
        lambda *refs: sketch_kernel(nz, ny, *refs),
        out_shape=jax.ShapeDtypeStruct((64, 512), bf16),
        in_specs=[pl.BlockSpec(memory_space=pltpu.VMEM)] * 2,
        out_specs=pl.BlockSpec(memory_space=pltpu.VMEM),
        scratch_shapes=[
            pltpu.VMEM((3, s_dev + 16, 512), bf16),
            pltpu.VMEM((s_dev, 512), bf16),
            pltpu.VMEM((4, s_dev, nz * 256), bf16),
            pltpu.VMEM((2, nz, 256, 256), bf16),
            pltpu.VMEM((2, 4, s_dev, 256), f32),
            pltpu.VMEM((2, 4, ny, 64, 256), bf16),
            pltpu.VMEM((2, 4, ny, 64, 256), bf16),
            pltpu.VMEM((2, 3, ny, 64, 256), bf16),
            pltpu.VMEM((2, 2, ny // 2, 64, 256), bf16),
            pltpu.VMEM((2, 2, ny, 64, 256), bf16),
            pltpu.VMEM((2, ny, 64, 256), f32),
            pltpu.VMEM((2, ny - 1, 64, 256), bf16),
            pltpu.VMEM((2, ny - 1, 64, 256), bf16),
            dma((2, 2, half, 2)), dma((2, 2, half, 2)),
            dma((6,)), dma((6,)),
            dma((2, 4)), dma((2, 4)),
            dma((2, 2)), dma((2, 2)),
            dma((2, 2, 2)), dma((2, 2, 2)),
            dma((2, ny - 1)), dma((2, ny - 1)),
        ],
        compiler_params=pltpu.CompilerParams(
            collective_id=0, has_side_effects=True, vmem_limit_bytes=56 << 20
        ),
        name="sketch",
    )(ge, blocks)


def pieces(value):
    hi = value.astype(bf16)
    return hi, (value - hi.astype(f32)).astype(bf16)


def times(a, b):
    (ah, al), (bh, bl) = a, b
    total = jnp.dot(ah, bh, preferred_element_type=f32) + jnp.dot(ah, bl, preferred_element_type=f32)
    return total + jnp.dot(al, bh, preferred_element_type=f32)


def whiten_kernel(
    nz, ny, samples, s_ref, out,
    sy, gram, gsend, gr, zsend, zr, zall, xall, yall, whole,
    yss, yrs, rss, rrs, zss, zrs, ass, ars, bss, brs, dss, drs, ess, ers,
):
    here = Place(nz, ny)
    z, x, y, c = here.z, here.x, here.y, here.c
    cx = [(dx, dc) for dx in range(NX) for dc in range(NC)][1:]
    ydev = {d: here.at(dy=d) for d in range(1, ny)}
    cxdev = {p: here.at(dx=p[0], dc=p[1]) for p in cx}
    zdev = {d: here.at(dz=d) for d in range(1, nz)}
    greet(list(ydev.values()) + list(cxdev.values()) + list(zdev.values()))
    started = []

    def remote(src, dst, ssem, rsem, to):
        return pltpu.make_async_remote_copy(
            src_ref=src, dst_ref=dst, send_sem=ssem, recv_sem=rsem, device_id=to, device_id_type=MESH
        )

    def go(copy):
        copy.start()
        started.append(copy)

    mine = s_ref[...]
    sy[0] = mine
    ys = [remote(sy.at[0], sy.at[d], yss.at[d - 1], yrs.at[d - 1], ydev[d]) for d in range(1, ny)]
    for copy in ys:
        go(copy)
    for copy in ys:
        copy.wait_recv()
    rows = ny * 64
    right = sy[...].reshape(rows, 512)
    left = sy[:, :, pl.ds(pl.multiple_of(128 * y, 128), 128)].reshape(rows, 128)
    gram[...] = lax.dot_general(left, right, (((0,), (0,)), ((), ())), preferred_element_type=f32)
    copies = []
    for n, (dx, dc) in enumerate(cx):
        at = 64 * lax.rem(c + dc, NC) + 16 * lax.rem(x + dx, NX)
        copies.append(
            remote(
                gram.at[pl.ds(pl.multiple_of(at, 16), 16)], gr.at[n], rss.at[n], rrs.at[n], cxdev[(dx, dc)]
            )
        )
        go(copies[-1])
    part = gram[pl.ds(pl.multiple_of(64 * c + 16 * x, 16), 16), :]
    for n, copy in enumerate(copies):
        copy.wait_recv()
        part = part + gr[n]
    for i in range(4):
        for j in range(4):
            zsend[4 * i + j] = part[4 * i : 4 * i + 4, 128 * j : 128 * j + 128]
    copies = []
    for d in range(1, nz):
        copies.append(
            remote(zsend.at[lax.rem(z + d, nz)], zr.at[d - 1], zss.at[d - 1], zrs.at[d - 1], zdev[d])
        )
        go(copies[-1])
    total = zsend[z]
    for d, copy in enumerate(copies):
        copy.wait_recv()
        total = total + zr[d]
    zall[z] = total
    copies = [remote(zall.at[z], zall.at[z], ass.at[d - 1], ars.at[d - 1], zdev[d]) for d in range(1, nz)]
    for copy in copies:
        go(copy)
    for d in range(1, nz):
        remote(
            zall.at[z], zall.at[lax.rem(z + nz - d, nz)], ass.at[d - 1], ars.at[d - 1], zdev[d]
        ).wait_recv()
    xall[x] = zall[...]
    copies = [remote(xall.at[x], xall.at[x], bss.at[d - 1], brs.at[d - 1], here.at(dx=d)) for d in range(1, NX)]
    for copy in copies:
        go(copy)
    for d in range(1, NX):
        remote(
            xall.at[x], xall.at[lax.rem(x + NX - d, NX)], bss.at[d - 1], brs.at[d - 1], here.at(dx=d)
        ).wait_recv()
    yall[y, c] = xall[...]
    copies = [remote(yall.at[y, c], yall.at[y, c], dss.at[d - 1], drs.at[d - 1], ydev[d]) for d in range(1, ny)]
    for copy in copies:
        go(copy)
    other = cxdev[(0, 1)]
    go(remote(yall.at[y, c], yall.at[y, c], ess.at[0], ers.at[0], other))
    for d in range(1, ny):
        from_y = lax.rem(y + ny - d, ny)
        remote(yall.at[y, c], yall.at[from_y, c], dss.at[d - 1], drs.at[d - 1], ydev[d]).wait_recv()
        go(remote(yall.at[from_y, c], yall.at[from_y, c], ess.at[d], ers.at[d], other))
    for d in range(ny):
        from_y = lax.rem(y + ny - d, ny)
        remote(yall.at[y, c], yall.at[from_y, 1 - c], ess.at[d], ers.at[d], other).wait_recv()
    for yy in range(ny):
        for cc in range(NC):
            for xx in range(NX):
                at = 128 * yy + 64 * cc + 16 * xx
                for i in range(4):
                    for j in range(4):
                        whole[at + 4 * i : at + 4 * i + 4, 128 * j : 128 * j + 128] = yall[yy, cc, xx, 4 * i + j]
    width = whole.shape[0]
    diag = lax.broadcasted_iota(jnp.int32, (width, width), 0) == lax.broadcasted_iota(jnp.int32, (width, width), 1)
    g = whole[...]
    g = jnp.where(diag, g + ridge * samples, g)
    scale = jnp.sum(jnp.where(diag, g, 0.0), keepdims=True) * (1.0 / width)
    w = g / scale
    v = mine.astype(f32)
    for step in range(root_steps):
        m = jnp.where(diag, 1.5 - 0.5 * w, -0.5 * w)
        mp = pieces(m)
        v = times(pieces(v), mp)
        if step + 1 < root_steps:
            w = times(pieces(times(pieces(w), mp)), mp)
    out[...] = v * (math.sqrt(samples) / jnp.sqrt(scale))
    for copy in started:
        copy.wait_send()


def whitened(sketch):
    nz, ny = sizes()
    samples = 512 * nz * NX
    dma = pltpu.SemaphoreType.DMA
    vmem = pltpu.VMEM
    n = NX * NC - 1
    return pl.pallas_call(
        lambda *refs: whiten_kernel(nz, ny, samples, *refs),
        out_shape=jax.ShapeDtypeStruct((64, 512), f32),
        in_specs=[pl.BlockSpec(memory_space=pltpu.VMEM)],
        out_specs=pl.BlockSpec(memory_space=pltpu.VMEM),
        scratch_shapes=[
            vmem((ny, 64, 512), bf16),
            vmem((128, 512), f32),
            vmem((16, 512), f32),
            vmem((n, 16, 512), f32),
            vmem((nz, 4, 128), f32),
            vmem((nz - 1, 4, 128), f32),
            vmem((nz, 4, 128), f32),
            vmem((NX, nz, 4, 128), f32),
            vmem((ny, NC, NX, nz, 4, 128), f32),
            vmem((512, 512), f32),
            dma((ny - 1,)), dma((ny - 1,)),
            dma((n,)), dma((n,)),
            dma((nz - 1,)), dma((nz - 1,)),
            dma((nz - 1,)), dma((nz - 1,)),
            dma((NX - 1,)), dma((NX - 1,)),
            dma((ny - 1,)), dma((ny - 1,)),
            dma((ny,)), dma((ny,)),
        ],
        compiler_params=pltpu.CompilerParams(
            collective_id=1, has_side_effects=True, vmem_limit_bytes=48 << 20
        ),
        name="whiten",
    )(sketch)


def local(grads, block_ids, probe):
    return whitened(sketch_rows(grads, block_ids, probe))


def solution(mesh):
    return jax.shard_map(
        local,
        mesh=mesh,
        in_specs=(P("feat", "dp", None, None), P("feat", "dp", None), P("dp", "feat", None, None)),
        out_specs=P(("dp", "feat"), None),
        check_vma=False,
    )
```

time: 688 us -> 152 us (0.22)
  the two profiles are of different devices: /device:TPU:23 before, /device:TPU:1 now
where the time goes in v1:
time: 152 us
  Pallas kernels  148 us (97%)
  local copies, waits for them, and re-layouts  2.61 us (2%)
  other arithmetic  1.52 us (1%)
    pallas_call x1, Pallas kernels, sketch_rows(): pl.pallas_call(lambda *refs: sketch_kernel(nz, ny, *refs), out_shape=jax....  96.4 us
    pallas_call x1, Pallas kernels, whitened(): pl.pallas_call(lambda *refs: whiten_kernel(nz, ny, samples, *refs), out_s...  51.4 us

profile of v1, /device:TPU:1, one launch (start us, length us, event | category | flops | bytes accessed | tf_op | source)
XLA Modules:
  0.0 152.0 jit_solution(9296748941652489157)
XLA Ops:
  0.0 0.7 fusion.2
  0.7 1.1 copy.6
  1.8 0.8 fusion.1.refs_0_
  2.6 96.4 %sketch.1.refs_0_ = bf16[64,512]{1,0:T(8,128)(2,1)} custom-call(bf16[528,512]{1,0:T(8,128)(2,1)} %fusion.1.refs_0_, bf16[256,512]{1,0:T(8,128)(2,1)} %bitcast.12), custom_call_target="tpu_custom_call" | custom-call | tf_op jit(solution)/shard_map/sketch/pallas_call | solution.py:285
  99.1 0.0 copy-start
  99.1 0.8 copy-done
  99.9 51.4 %whiten.1 = f32[64,512]{1,0:T(8,128)S(1)} custom-call(bf16[64,512]{1,0:T(8,128)(2,1)S(1)} %copy-done), custom_call_target="tpu_custom_call" | custom-call | tf_op jit(solution)/shard_map/whiten/pallas_call | solution.py:449
  151.3 0.7 copy.8
Async XLA Ops:
  99.1 0.8 copy-start

commit v2 on v1

--- a/solution.py
+++ b/solution.py
@@ -34,17 +34,23 @@
         return {"dp": z * NX + x, "feat": y * NC + c}
 
 
-def greet(others):
-    barrier = pltpu.get_barrier_semaphore()
-    for other in others:
-        pl.semaphore_signal(barrier, inc=1, device_id=other, device_id_type=MESH)
-    pl.semaphore_wait(barrier, len(others))
-
-
-def sketch_kernel(
-    nz, ny, ge, probe, out,
-    gx, codes, dense, pbuf, acc, csend, crecv, xs, xo, xr, rows, ys, yr,
+def pieces(value):
+    hi = value.astype(bf16)
+    return hi, (value - hi.astype(f32)).astype(bf16)
+
+
+def times(a, b):
+    (ah, al), (bh, bl) = a, b
+    total = jnp.dot(ah, bh, preferred_element_type=f32) + jnp.dot(ah, bl, preferred_element_type=f32)
+    return total + jnp.dot(al, bh, preferred_element_type=f32)
+
+
+def kernel(
+    nz, ny, samples, grads, ids, probe, out,
+    ge, gx, codes, dense, pbuf, acc, csend, crecv, xs, xo, xr, rows, ys, yr,
+    sy, gram, gr, zsend, zr, zall, xall, yall, whole,
     zss, zrs, xss, xrs, css, crs, oss, ors, qss, qrs, yss, yrs,
+    sss, srs, rss, rrs, ess, ers, fss, frs, ass, ars, bss, brs, dss, drs,
 ):
     here = Place(nz, ny)
     z, x, y, c = here.z, here.x, here.y, here.c
@@ -53,7 +59,23 @@
     right_z, left_z = here.at(dz=1), here.at(dz=-1)
     right_x, left_x = here.at(dx=1), here.at(dx=-1)
     other_core = here.at(dc=1)
-    greet([right_z, left_z, right_x, left_x, other_core] + [here.at(dy=d) for d in range(1, ny)])
+    ydev = {d: here.at(dy=d) for d in range(1, ny)}
+    near = [right_z, left_z, right_x, left_x, other_core] + list(ydev.values())
+    barrier = pltpu.get_barrier_semaphore()
+    for other in near:
+        pl.semaphore_signal(barrier, inc=1, device_id=other, device_id_type=MESH)
+
+    for h in range(2):
+        pbuf[h, 0] = probe[:, pl.ds(256 * h, 256)]
+    row = lax.broadcasted_iota(jnp.int32, (256, 256), 0)
+    picked = 4 * lax.rem(row, 64) + row // 64 == lax.broadcasted_iota(jnp.int32, (256, 256), 1)
+    pick = picked.astype(f32).astype(bf16)
+    for i in range(s_dev // 64):
+        part = jnp.dot(pick, grads[256 * i : 256 * i + 256], preferred_element_type=f32).astype(bf16)
+        for k in range(4):
+            ge[64 * i : 64 * i + 64, 128 * k : 128 * k + 128] = part[64 * k : 64 * k + 64]
+    ge[s_dev:, :] = jnp.concatenate([ids[...].astype(f32), jnp.zeros((12, s_dev), f32)], axis=0).astype(bf16)
+    pl.semaphore_wait(barrier, len(near))
 
     def remote(src, dst, ssem, rsem, to):
         return pltpu.make_async_remote_copy(
@@ -78,13 +100,12 @@
     def zsent(way, s, w):
         return s < half - 1 or (s == half - 1 and w == way)
 
-    def arrive(h, s):
-        for w in range(2):
-            for way in range(2):
-                if zsent(way, s, w):
-                    zcopy(way, h, s, w).wait_recv()
-                    if s + 1 < half and zsent(way, s + 1, w):
-                        go(zcopy(way, h, s + 1, w))
+    def arrive(h, s, w):
+        for way in range(2):
+            if zsent(way, s, w):
+                zcopy(way, h, s, w).wait_recv()
+                if s + 1 < half and zsent(way, s + 1, w):
+                    go(zcopy(way, h, s + 1, w))
 
     def own(h):
         for w in range(2):
@@ -101,7 +122,7 @@
         "fb": remote(gx.at[1, hi], gx.at[2, hi], xss.at[5], xrs.at[5], left_x),
     }
 
-    def expand(t):
+    def encode(t):
         src = ge if t == 0 else gx.at[t - 1]
         ids = src[pl.ds(s_dev, 16), :].astype(jnp.int32)
         m = lax.rem(z + nz - ids // 8, nz)
@@ -113,7 +134,12 @@
             code, picks, (((0,), (0,)), ((), ())), preferred_element_type=f32
         ).astype(bf16)
 
-        @pl.loop(0, s_dev // 32)
+    def expand(t, part):
+        src = ge if t == 0 else gx.at[t - 1]
+        if part == 0:
+            encode(t)
+
+        @pl.loop(part * s_dev // 64, (part + 1) * s_dev // 64)
         def _(i):
             r = pl.ds(pl.multiple_of(i * 32, 32), 32)
             g = [src[r, pl.ds(128 * k, 128)] for k in range(4)]
@@ -166,7 +192,11 @@
         )
 
     def ycopy(h, d):
-        return remote(ys.at[h, d - 1], yr.at[h, d - 1], yss.at[h, d - 1], yrs.at[h, d - 1], here.at(dy=d))
+        return remote(ys.at[h, d - 1], yr.at[h, d - 1], yss.at[h, d - 1], yrs.at[h, d - 1], ydev[d])
+
+    def scopy(h, d):
+        cols = pl.ds(256 * h, 256)
+        return remote(sy.at[0, :, cols], sy.at[d, :, cols], sss.at[h, d - 1], srs.at[h, d - 1], ydev[d])
 
     def far(h):
         ccopy(h, 3).wait_recv()
@@ -175,7 +205,7 @@
         go(ocopy(h, 0))
         go(ocopy(h, 1))
 
-    def near(h):
+    def beside(h):
         ccopy(h, 2).wait_recv()
         for yy in bottoms:
             xs[h, 1, yy] = both(h, 2, yy).astype(bf16)
@@ -211,154 +241,84 @@
         for d in range(1, ny):
             ycopy(h, d).wait_recv()
             total = total + yr[h, d - 1].astype(f32)
-        out[:, pl.ds(256 * h, 256)] = total.astype(bf16)
-
-    for h in range(2):
-        pbuf[h, 0] = probe[:, pl.ds(256 * h, 256)]
-    own(0)
-    for name in ("ra", "lb", "rb", "la"):
-        go(xc[name])
-    expand(0)
-    whole = [(0, nz)]
+        cols = pl.ds(256 * h, 256)
+        sy[0, :, cols] = total.astype(bf16)
+        for d in range(1, ny):
+            go(scopy(h, d))
+
+    def pass_a():
+        xc["ra"].wait_recv()
+        go(xc["fa"])
+
+    def pass_b():
+        xc["lb"].wait_recv()
+        go(xc["fb"])
+
+    def last(h, t):
+        product(h, t, late, False)
+        give_core(h, t)
+
+    def first(h, t):
+        product(h, t, early, True)
+
+    def samples_here(*names):
+        for name in names:
+            xc[name].wait_recv()
+
+    lag = 2
     early, late = [(0, 6), (11, nz)], [(6, 11)]
-    for s in range(half):
-        arrive(0, s)
-        if s == 1:
-            xc["ra"].wait_recv()
-            go(xc["fa"])
-            xc["lb"].wait_recv()
-            go(xc["fb"])
-        if s == 3:
-            xc["rb"].wait_recv()
-            expand(1)
-        if s == 4:
-            xc["la"].wait_recv()
-            expand(2)
-        if s == half - 2:
-            own(1)
-    xc["fa"].wait_recv()
-    xc["fb"].wait_recv()
-    expand(3)
-    for s in range(half):
-        if s == half - 1:
-            product(1, 0, early, True)
-        arrive(1, s)
-        if s < 4:
-            product(0, 3 - s, whole, True)
-            give_core(0, 3 - s)
-        if s == 2:
-            far(0)
-        if s == 3:
-            near(0)
-        if s == 4:
+    work = {
+        1: [pass_a, pass_b],
+        3: [
+            lambda: (samples_here("rb"), expand(1, 0)), lambda: expand(1, 1),
+            lambda: (samples_here("la"), expand(2, 0)), lambda: expand(2, 1),
+        ],
+        4: [lambda: None, lambda: None, lambda: (samples_here("fa", "fb"), expand(3, 0)), lambda: expand(3, 1)],
+        5: [lambda t=t: first(0, t) for t in (3, 2, 1, 0)],
+        7: [lambda: first(1, 3), lambda: first(1, 2), lambda: None, lambda: None]
+        + [lambda t=t: last(0, t) for t in (3, 2, 1, 0)],
+        8: [lambda: far(0), lambda: beside(0), lambda: first(1, 1), lambda: first(1, 0)],
+    }
+    for e in range(half + lag):
+        todo = list(work.get(e, []))
+        parts = [h for h in range(2) if 0 <= e - lag * h < half]
+        for h in parts:
+            if e == lag * h:
+                own(h)
+        if e == 0:
+            for name in ("ra", "lb", "rb", "la"):
+                go(xc[name])
+            expand(0, 0)
+            expand(0, 1)
+        if e == half + lag - 1:
             joined(0)
             home(0)
-        if s == 5:
-            finish(0)
-            product(1, 3, early, True)
-        if s == 6:
-            product(1, 2, early, True)
-            product(1, 1, early, True)
-    for t in (3, 2, 1, 0):
-        product(1, t, late, False)
-        give_core(1, t)
-        if t == 2:
-            far(1)
-        if t == 0:
-            near(1)
+        for w in range(2):
+            for h in parts:
+                arrive(h, e - lag * h, w)
+                if todo:
+                    todo.pop(0)()
+        for task in todo:
+            task()
+    last(1, 3)
+    last(1, 2)
+    far(1)
+    last(1, 1)
+    last(1, 0)
+    beside(1)
+    finish(0)
     joined(1)
     home(1)
     finish(1)
-    for copy in started:
-        copy.wait_send()
-
-
-def sketch_rows(grads, block_ids, probe):
-    nz, ny = sizes()
-    s_dev = grads.shape[1]
-    values = grads[0].reshape(s_dev, 512)
-    ids = jnp.pad(block_ids[0].T.astype(f32).astype(bf16), ((0, 12), (0, 0)))
-    ge = jnp.concatenate([values, ids], axis=0)
-    blocks = probe.reshape(256, 512)
-    half = nz // 2
-    dma = pltpu.SemaphoreType.DMA
-    return pl.pallas_call(
-        lambda *refs: sketch_kernel(nz, ny, *refs),
-        out_shape=jax.ShapeDtypeStruct((64, 512), bf16),
-        in_specs=[pl.BlockSpec(memory_space=pltpu.VMEM)] * 2,
-        out_specs=pl.BlockSpec(memory_space=pltpu.VMEM),
-        scratch_shapes=[
-            pltpu.VMEM((3, s_dev + 16, 512), bf16),
-            pltpu.VMEM((s_dev, 512), bf16),
-            pltpu.VMEM((4, s_dev, nz * 256), bf16),
-            pltpu.VMEM((2, nz, 256, 256), bf16),
-            pltpu.VMEM((2, 4, s_dev, 256), f32),
-            pltpu.VMEM((2, 4, ny, 64, 256), bf16),
-            pltpu.VMEM((2, 4, ny, 64, 256), bf16),
-            pltpu.VMEM((2, 3, ny, 64, 256), bf16),
-            pltpu.VMEM((2, 2, ny // 2, 64, 256), bf16),
-            pltpu.VMEM((2, 2, ny, 64, 256), bf16),
-            pltpu.VMEM((2, ny, 64, 256), f32),
-            pltpu.VMEM((2, ny - 1, 64, 256), bf16),
-            pltpu.VMEM((2, ny - 1, 64, 256), bf16),
-            dma((2, 2, half, 2)), dma((2, 2, half, 2)),
-            dma((6,)), dma((6,)),
-            dma((2, 4)), dma((2, 4)),
-            dma((2, 2)), dma((2, 2)),
-            dma((2, 2, 2)), dma((2, 2, 2)),
-            dma((2, ny - 1)), dma((2, ny - 1)),
-        ],
-        compiler_params=pltpu.CompilerParams(
-            collective_id=0, has_side_effects=True, vmem_limit_bytes=56 << 20
-        ),
-        name="sketch",
-    )(ge, blocks)
-
-
-def pieces(value):
-    hi = value.astype(bf16)
-    return hi, (value - hi.astype(f32)).astype(bf16)
-
-
-def times(a, b):
-    (ah, al), (bh, bl) = a, b
-    total = jnp.dot(ah, bh, preferred_element_type=f32) + jnp.dot(ah, bl, preferred_element_type=f32)
-    return total + jnp.dot(al, bh, preferred_element_type=f32)
-
-
-def whiten_kernel(
-    nz, ny, samples, s_ref, out,
-    sy, gram, gsend, gr, zsend, zr, zall, xall, yall, whole,
-    yss, yrs, rss, rrs, zss, zrs, ass, ars, bss, brs, dss, drs, ess, ers,
-):
-    here = Place(nz, ny)
-    z, x, y, c = here.z, here.x, here.y, here.c
+
+    for h in range(2):
+        for d in range(1, ny):
+            scopy(h, d).wait_recv()
     cx = [(dx, dc) for dx in range(NX) for dc in range(NC)][1:]
-    ydev = {d: here.at(dy=d) for d in range(1, ny)}
     cxdev = {p: here.at(dx=p[0], dc=p[1]) for p in cx}
     zdev = {d: here.at(dz=d) for d in range(1, nz)}
-    greet(list(ydev.values()) + list(cxdev.values()) + list(zdev.values()))
-    started = []
-
-    def remote(src, dst, ssem, rsem, to):
-        return pltpu.make_async_remote_copy(
-            src_ref=src, dst_ref=dst, send_sem=ssem, recv_sem=rsem, device_id=to, device_id_type=MESH
-        )
-
-    def go(copy):
-        copy.start()
-        started.append(copy)
-
-    mine = s_ref[...]
-    sy[0] = mine
-    ys = [remote(sy.at[0], sy.at[d], yss.at[d - 1], yrs.at[d - 1], ydev[d]) for d in range(1, ny)]
-    for copy in ys:
-        go(copy)
-    for copy in ys:
-        copy.wait_recv()
-    rows = ny * 64
-    right = sy[...].reshape(rows, 512)
-    left = sy[:, :, pl.ds(pl.multiple_of(128 * y, 128), 128)].reshape(rows, 128)
+    right = sy[...].reshape(ny * 64, 512)
+    left = sy[:, :, pl.ds(pl.multiple_of(128 * y, 128), 128)].reshape(ny * 64, 128)
     gram[...] = lax.dot_general(left, right, (((0,), (0,)), ((), ())), preferred_element_type=f32)
     copies = []
     for n, (dx, dc) in enumerate(cx):
@@ -379,7 +339,7 @@
     copies = []
     for d in range(1, nz):
         copies.append(
-            remote(zsend.at[lax.rem(z + d, nz)], zr.at[d - 1], zss.at[d - 1], zrs.at[d - 1], zdev[d])
+            remote(zsend.at[lax.rem(z + d, nz)], zr.at[d - 1], ess.at[d - 1], ers.at[d - 1], zdev[d])
         )
         go(copies[-1])
     total = zsend[z]
@@ -407,14 +367,14 @@
     for copy in copies:
         go(copy)
     other = cxdev[(0, 1)]
-    go(remote(yall.at[y, c], yall.at[y, c], ess.at[0], ers.at[0], other))
+    go(remote(yall.at[y, c], yall.at[y, c], fss.at[0], frs.at[0], other))
     for d in range(1, ny):
         from_y = lax.rem(y + ny - d, ny)
         remote(yall.at[y, c], yall.at[from_y, c], dss.at[d - 1], drs.at[d - 1], ydev[d]).wait_recv()
-        go(remote(yall.at[from_y, c], yall.at[from_y, c], ess.at[d], ers.at[d], other))
+        go(remote(yall.at[from_y, c], yall.at[from_y, c], fss.at[d], frs.at[d], other))
     for d in range(ny):
         from_y = lax.rem(y + ny - d, ny)
-        remote(yall.at[y, c], yall.at[from_y, 1 - c], ess.at[d], ers.at[d], other).wait_recv()
+        remote(yall.at[y, c], yall.at[from_y, 1 - c], fss.at[d], frs.at[d], other).wait_recv()
     for yy in range(ny):
         for cc in range(NC):
             for xx in range(NX):
@@ -428,7 +388,7 @@
     g = jnp.where(diag, g + ridge * samples, g)
     scale = jnp.sum(jnp.where(diag, g, 0.0), keepdims=True) * (1.0 / width)
     w = g / scale
-    v = mine.astype(f32)
+    v = sy[0].astype(f32)
     for step in range(root_steps):
         m = jnp.where(diag, 1.5 - 0.5 * w, -0.5 * w)
         mp = pieces(m)
@@ -440,21 +400,35 @@
         copy.wait_send()
 
 
-def whitened(sketch):
+def local(grads, block_ids, probe):
     nz, ny = sizes()
-    samples = 512 * nz * NX
+    s_dev = grads.shape[1]
+    half = nz // 2
+    n = NX * NC - 1
     dma = pltpu.SemaphoreType.DMA
     vmem = pltpu.VMEM
-    n = NX * NC - 1
     return pl.pallas_call(
-        lambda *refs: whiten_kernel(nz, ny, samples, *refs),
+        lambda *refs: kernel(nz, ny, s_dev * nz * NX, *refs),
         out_shape=jax.ShapeDtypeStruct((64, 512), f32),
-        in_specs=[pl.BlockSpec(memory_space=pltpu.VMEM)],
+        in_specs=[pl.BlockSpec(memory_space=pltpu.VMEM)] * 3,
         out_specs=pl.BlockSpec(memory_space=pltpu.VMEM),
         scratch_shapes=[
+            vmem((s_dev + 16, 512), bf16),
+            vmem((3, s_dev + 16, 512), bf16),
+            vmem((s_dev, 512), bf16),
+            vmem((4, s_dev, nz * 256), bf16),
+            vmem((2, nz, 256, 256), bf16),
+            vmem((2, 4, s_dev, 256), f32),
+            vmem((2, 4, ny, 64, 256), bf16),
+            vmem((2, 4, ny, 64, 256), bf16),
+            vmem((2, 3, ny, 64, 256), bf16),
+            vmem((2, 2, ny // 2, 64, 256), bf16),
+            vmem((2, 2, ny, 64, 256), bf16),
+            vmem((2, ny, 64, 256), f32),
+            vmem((2, ny - 1, 64, 256), bf16),
+            vmem((2, ny - 1, 64, 256), bf16),
             vmem((ny, 64, 512), bf16),
             vmem((128, 512), f32),
-            vmem((16, 512), f32),
             vmem((n, 16, 512), f32),
             vmem((nz, 4, 128), f32),
             vmem((nz - 1, 4, 128), f32),
@@ -462,23 +436,25 @@
             vmem((NX, nz, 4, 128), f32),
             vmem((ny, NC, NX, nz, 4, 128), f32),
             vmem((512, 512), f32),
-            dma((ny - 1,)), dma((ny - 1,)),
+            dma((2, 2, half, 2)), dma((2, 2, half, 2)),
+            dma((6,)), dma((6,)),
+            dma((2, 4)), dma((2, 4)),
+            dma((2, 2)), dma((2, 2)),
+            dma((2, 2, 2)), dma((2, 2, 2)),
+            dma((2, ny - 1)), dma((2, ny - 1)),
+            dma((2, ny - 1)), dma((2, ny - 1)),
             dma((n,)), dma((n,)),
             dma((nz - 1,)), dma((nz - 1,)),
+            dma((ny,)), dma((ny,)),
             dma((nz - 1,)), dma((nz - 1,)),
             dma((NX - 1,)), dma((NX - 1,)),
             dma((ny - 1,)), dma((ny - 1,)),
-            dma((ny,)), dma((ny,)),
         ],
         compiler_params=pltpu.CompilerParams(
-            collective_id=1, has_side_effects=True, vmem_limit_bytes=48 << 20
+            collective_id=0, has_side_effects=True, vmem_limit_bytes=58 << 20
         ),
         name="whiten",
-    )(sketch)
-
-
-def local(grads, block_ids, probe):
-    return whitened(sketch_rows(grads, block_ids, probe))
+    )(grads.reshape(s_dev * 4, 128), block_ids[0].T, probe.reshape(256, 512))
 
 
 def solution(mesh):

time: 152 us -> 131 us (0.86)
  Pallas kernels: 148 us -> 129 us
  other arithmetic: 1.52 us -> 0 us
    pallas_call x2 -> x1, Pallas kernels: 148 us -> 129 us  [local(): pl.pallas_call(lambda *refs: kernel(nz, ny, s_dev * nz * NX, *refs), out_...]
where the time goes in v2:
time: 131 us
  Pallas kernels  129 us (98%)
  local copies, waits for them, and re-layouts  1.57 us (1%)
    pallas_call x1, Pallas kernels, local(): pl.pallas_call(lambda *refs: kernel(nz, ny, s_dev * nz * NX, *refs), out_...  129 us

profile of v2, /device:TPU:1, one launch (start us, length us, event | category | flops | bytes accessed | tf_op | source)
XLA Modules:
  0.0 130.5 jit_solution(10151537713281030053)
XLA Ops:
  0.0 128.9 %whiten.1 = f32[64,512]{1,0:T(8,128)} custom-call(bf16[2048,128]{1,0:T(8,128)(2,1)} %bitcast.5, s32[4,512]{1,0:T(4,128)} %bitcast.7, bf16[256,512]{1,0:T(8,128)(2,1)} %bitcast.6), custom_call_target="tpu_custom_call" | custom-call | tf_op jit(solution)/shard_map/whiten/pallas_call | solution.py:410
  128.9 1.6 %copy.5 = f32[64,512]{1,0:T(8,128)} copy(f32[64,512]{1,0:T(8,128)} %whiten.1) | data formatting | bytes 262144

commit v3 on v2

--- a/solution.py
+++ b/solution.py
@@ -47,9 +47,9 @@
 
 def kernel(
     nz, ny, samples, grads, ids, probe, out,
-    ge, gx, codes, dense, pbuf, acc, csend, crecv, xs, xo, xr, rows, ys, yr,
-    sy, gram, gr, zsend, zr, zall, xall, yall, whole,
-    zss, zrs, xss, xrs, css, crs, oss, ors, qss, qrs, yss, yrs,
+    ge, gx, codes, dense, pbuf, acc, csend, crecv, ps, pr,
+    sy, gram, gr, qs, qr, qall, ball, yall, whole,
+    zss, zrs, xss, xrs, css, crs, pss, prs,
     sss, srs, rss, rrs, ess, ers, fss, frs, ass, ars, bss, brs, dss, drs,
 ):
     here = Place(nz, ny)
@@ -60,7 +60,8 @@
     right_x, left_x = here.at(dx=1), here.at(dx=-1)
     other_core = here.at(dc=1)
     ydev = {d: here.at(dy=d) for d in range(1, ny)}
-    near = [right_z, left_z, right_x, left_x, other_core] + list(ydev.values())
+    plane = {(dx, dy): here.at(dx=dx, dy=dy) for dx in (2, 1, 3, 0) for dy in range(ny) if (dx, dy) != (0, 0)}
+    near = [right_z, left_z, other_core] + list(plane.values())
     barrier = pltpu.get_barrier_semaphore()
     for other in near:
         pl.semaphore_signal(barrier, inc=1, device_id=other, device_id_type=MESH)
@@ -171,76 +172,31 @@
             csend[h, t, yy] = acc[h, t, pl.ds(pl.multiple_of(128 * yy + 64 * (1 - c), 64), 64), :].astype(bf16)
         go(ccopy(h, t))
 
-    def both(h, t, yy):
-        mine = acc[h, t, pl.ds(pl.multiple_of(128 * yy + 64 * c, 64), 64), :]
-        return mine + crecv[h, t, yy].astype(f32)
-
-    top, bottom = pl.ds(0, ny // 2), pl.ds(ny // 2, ny // 2)
-    tops, bottoms = range(ny // 2), range(ny // 2, ny)
-
-    def ocopy(h, way):
-        part = top if way == 0 else bottom
-        return remote(
-            xs.at[h, 2, part], xo.at[h, way], oss.at[h, way], ors.at[h, way], right_x if way == 0 else left_x
-        )
-
-    def qcopy(h, way, part):
-        span = top if part == 0 else bottom
-        return remote(
-            xs.at[h, 1 - way, span], xr.at[h, way, span], qss.at[h, way, part], qrs.at[h, way, part],
-            right_x if way == 0 else left_x,
-        )
-
-    def ycopy(h, d):
-        return remote(ys.at[h, d - 1], yr.at[h, d - 1], yss.at[h, d - 1], yrs.at[h, d - 1], ydev[d])
+    def pcopy(h, dx, dy):
+        return remote(ps.at[h, dx, dy], pr.at[h, dx, dy], pss.at[h, dx, dy], prs.at[h, dx, dy], plane[(dx, dy)])
 
     def scopy(h, d):
         cols = pl.ds(256 * h, 256)
         return remote(sy.at[0, :, cols], sy.at[d, :, cols], sss.at[h, d - 1], srs.at[h, d - 1], ydev[d])
 
-    def far(h):
-        ccopy(h, 3).wait_recv()
-        for yy in range(ny):
-            xs[h, 2, yy] = both(h, 3, yy).astype(bf16)
-        go(ocopy(h, 0))
-        go(ocopy(h, 1))
-
-    def beside(h):
-        ccopy(h, 2).wait_recv()
-        for yy in bottoms:
-            xs[h, 1, yy] = both(h, 2, yy).astype(bf16)
-        go(qcopy(h, 0, 1))
-        ccopy(h, 1).wait_recv()
-        for yy in tops:
-            xs[h, 0, yy] = both(h, 1, yy).astype(bf16)
-        go(qcopy(h, 1, 0))
-
-    def joined(h):
-        ocopy(h, 0).wait_recv()
-        for yy in tops:
-            xs[h, 1, yy] = (both(h, 2, yy) + xo[h, 0, yy].astype(f32)).astype(bf16)
-        go(qcopy(h, 0, 0))
-        ocopy(h, 1).wait_recv()
-        for yy in bottoms:
-            xs[h, 0, yy] = (both(h, 1, yy) + xo[h, 1, yy - ny // 2].astype(f32)).astype(bf16)
-        go(qcopy(h, 1, 1))
-
-    def home(h):
-        ccopy(h, 0).wait_recv()
-        for way in range(2):
-            for part in range(2):
-                qcopy(h, way, part).wait_recv()
-        for yy in range(ny):
-            rows[h, yy] = both(h, 0, yy) + xr[h, 0, yy].astype(f32) + xr[h, 1, yy].astype(f32)
-        for d in range(1, ny):
-            ys[h, d - 1] = rows[h, lax.rem(y + d, ny)].astype(bf16)
-            go(ycopy(h, d))
+    def spread(h, t):
+        dx = (0, 3, 1, 2)[t]
+        ccopy(h, t).wait_recv()
+        for dy in reversed(range(ny)):
+            yy = lax.rem(y + dy, ny)
+            mine = acc[h, t, pl.ds(pl.multiple_of(128 * yy + 64 * c, 64), 64), :]
+            both = mine + crecv[h, t, yy].astype(f32)
+            if (dx, dy) == (0, 0):
+                acc[h, 0, 0:64] = both
+            else:
+                ps[h, dx, dy] = both.astype(bf16)
+                go(pcopy(h, dx, dy))
 
     def finish(h):
-        total = rows[h, y]
-        for d in range(1, ny):
-            ycopy(h, d).wait_recv()
-            total = total + yr[h, d - 1].astype(f32)
+        total = acc[h, 0, 0:64]
+        for dx, dy in plane:
+            pcopy(h, dx, dy).wait_recv()
+            total = total + pr[h, dx, dy].astype(f32)
         cols = pl.ds(256 * h, 256)
         sy[0, :, cols] = total.astype(bf16)
         for d in range(1, ny):
@@ -277,7 +233,7 @@
         5: [lambda t=t: first(0, t) for t in (3, 2, 1, 0)],
         7: [lambda: first(1, 3), lambda: first(1, 2), lambda: None, lambda: None]
         + [lambda t=t: last(0, t) for t in (3, 2, 1, 0)],
-        8: [lambda: far(0), lambda: beside(0), lambda: first(1, 1), lambda: first(1, 0)],
+        8: [lambda: spread(0, 3), lambda: first(1, 1), lambda: spread(0, 2), lambda: first(1, 0), lambda: (spread(0, 1), spread(0, 0))],
     }
     for e in range(half + lag):
         todo = list(work.get(e, []))
@@ -290,9 +246,6 @@
                 go(xc[name])
             expand(0, 0)
             expand(0, 1)
-        if e == half + lag - 1:
-            joined(0)
-            home(0)
         for w in range(2):
             for h in parts:
                 arrive(h, e - lag * h, w)
@@ -302,13 +255,13 @@
             task()
     last(1, 3)
     last(1, 2)
-    far(1)
+    spread(1, 3)
     last(1, 1)
+    spread(1, 2)
     last(1, 0)
-    beside(1)
+    spread(1, 1)
+    spread(1, 0)
     finish(0)
-    joined(1)
-    home(1)
     finish(1)
 
     for h in range(2):
@@ -316,7 +269,6 @@
             scopy(h, d).wait_recv()
     cx = [(dx, dc) for dx in range(NX) for dc in range(NC)][1:]
     cxdev = {p: here.at(dx=p[0], dc=p[1]) for p in cx}
-    zdev = {d: here.at(dz=d) for d in range(1, nz)}
     right = sy[...].reshape(ny * 64, 512)
     left = sy[:, :, pl.ds(pl.multiple_of(128 * y, 128), 128)].reshape(ny * 64, 128)
     gram[...] = lax.dot_general(left, right, (((0,), (0,)), ((), ())), preferred_element_type=f32)
@@ -333,55 +285,58 @@
     for n, copy in enumerate(copies):
         copy.wait_recv()
         part = part + gr[n]
+    zpart, zat = z // 4, lax.rem(z, 4)
     for i in range(4):
-        for j in range(4):
-            zsend[4 * i + j] = part[4 * i : 4 * i + 4, 128 * j : 128 * j + 128]
+        qs[i] = part[4 * i : 4 * i + 4]
+
+    def zpeer(d):
+        return {"dp": (4 * zpart + lax.rem(zat + d, 4)) * NX + x, "feat": y * NC + c}
+
     copies = []
-    for d in range(1, nz):
-        copies.append(
-            remote(zsend.at[lax.rem(z + d, nz)], zr.at[d - 1], ess.at[d - 1], ers.at[d - 1], zdev[d])
-        )
+    for d in range(1, 4):
+        copies.append(remote(qs.at[lax.rem(zat + d, 4)], qr.at[d - 1], ess.at[d - 1], ers.at[d - 1], zpeer(d)))
         go(copies[-1])
-    total = zsend[z]
+    total = qs[zat]
     for d, copy in enumerate(copies):
         copy.wait_recv()
-        total = total + zr[d]
-    zall[z] = total
-    copies = [remote(zall.at[z], zall.at[z], ass.at[d - 1], ars.at[d - 1], zdev[d]) for d in range(1, nz)]
-    for copy in copies:
-        go(copy)
-    for d in range(1, nz):
-        remote(
-            zall.at[z], zall.at[lax.rem(z + nz - d, nz)], ass.at[d - 1], ars.at[d - 1], zdev[d]
-        ).wait_recv()
-    xall[x] = zall[...]
-    copies = [remote(xall.at[x], xall.at[x], bss.at[d - 1], brs.at[d - 1], here.at(dx=d)) for d in range(1, NX)]
-    for copy in copies:
-        go(copy)
-    for d in range(1, NX):
-        remote(
-            xall.at[x], xall.at[lax.rem(x + NX - d, NX)], bss.at[d - 1], brs.at[d - 1], here.at(dx=d)
-        ).wait_recv()
-    yall[y, c] = xall[...]
-    copies = [remote(yall.at[y, c], yall.at[y, c], dss.at[d - 1], drs.at[d - 1], ydev[d]) for d in range(1, ny)]
-    for copy in copies:
-        go(copy)
-    other = cxdev[(0, 1)]
-    go(remote(yall.at[y, c], yall.at[y, c], fss.at[0], frs.at[0], other))
-    for d in range(1, ny):
-        from_y = lax.rem(y + ny - d, ny)
-        remote(yall.at[y, c], yall.at[from_y, c], dss.at[d - 1], drs.at[d - 1], ydev[d]).wait_recv()
-        go(remote(yall.at[from_y, c], yall.at[from_y, c], fss.at[d], frs.at[d], other))
-    for d in range(ny):
-        from_y = lax.rem(y + ny - d, ny)
-        remote(yall.at[y, c], yall.at[from_y, 1 - c], fss.at[d], frs.at[d], other).wait_recv()
+        total = total + qr[d]
+    parts = nz // 4
+    qall[zpart] = total
+    for d in range(1, parts):
+        go(remote(qall.at[zpart], qall.at[zpart], ass.at[d - 1], ars.at[d - 1], here.at(dz=4 * d)))
+    for d in range(1, parts):
+        source = lax.rem(zpart + parts - d, parts)
+        remote(qall.at[zpart], qall.at[source], ass.at[d - 1], ars.at[d - 1], here.at(dz=4 * d)).wait_recv()
+    total = qall[0]
+    for i in range(1, parts):
+        total = total + qall[i]
+    ball[zat] = total
+    for d in range(1, 4):
+        go(remote(ball.at[zat], ball.at[zat], bss.at[d - 1], brs.at[d - 1], zpeer(d)))
+    for d in range(1, 4):
+        source = lax.rem(zat + 4 - d, 4)
+        remote(ball.at[zat], ball.at[source], bss.at[d - 1], brs.at[d - 1], zpeer(d)).wait_recv()
+    yall[c, y, x] = ball[...]
+    for dx, dy in plane:
+        go(remote(ball, yall.at[c, y, x], dss.at[dx, dy], drs.at[dx, dy], plane[(dx, dy)]))
+    for dy in (0, 1, 3, 2):
+        from_y = lax.rem(y + ny - dy, ny)
+        for dx in range(NX):
+            if (dx, dy) != (0, 0):
+                from_x = lax.rem(x + NX - dx, NX)
+                remote(
+                    ball, yall.at[c, from_y, from_x], dss.at[dx, dy], drs.at[dx, dy], plane[(dx, dy)]
+                ).wait_recv()
+        go(remote(yall.at[c, from_y], yall.at[c, from_y], fss.at[dy], frs.at[dy], other_core))
+    for dy in range(ny):
+        from_y = lax.rem(y + ny - dy, ny)
+        remote(yall.at[c, from_y], yall.at[1 - c, from_y], fss.at[dy], frs.at[dy], other_core).wait_recv()
     for yy in range(ny):
         for cc in range(NC):
             for xx in range(NX):
                 at = 128 * yy + 64 * cc + 16 * xx
                 for i in range(4):
-                    for j in range(4):
-                        whole[at + 4 * i : at + 4 * i + 4, 128 * j : 128 * j + 128] = yall[yy, cc, xx, 4 * i + j]
+                    whole[at + 4 * i : at + 4 * i + 4, :] = yall[cc, yy, xx, i]
     width = whole.shape[0]
     diag = lax.broadcasted_iota(jnp.int32, (width, width), 0) == lax.broadcasted_iota(jnp.int32, (width, width), 1)
     g = whole[...]
@@ -389,12 +344,14 @@
     scale = jnp.sum(jnp.where(diag, g, 0.0), keepdims=True) * (1.0 / width)
     w = g / scale
     v = sy[0].astype(f32)
-    for step in range(root_steps):
-        m = jnp.where(diag, 1.5 - 0.5 * w, -0.5 * w)
-        mp = pieces(m)
+    for step in range(root_steps - 1):
+        wp = pieces(w)
+        mp = pieces(jnp.where(diag, 1.5 - 0.5 * w, -0.5 * w))
         v = times(pieces(v), mp)
-        if step + 1 < root_steps:
-            w = times(pieces(times(pieces(w), mp)), mp)
+        if step + 2 < root_steps:
+            w = times(pieces(times(wp, mp)), mp)
+    u = times(pieces(times(pieces(times(pieces(v), wp)), mp)), mp)
+    v = 1.5 * v - 0.5 * u
     out[...] = v * (math.sqrt(samples) / jnp.sqrt(scale))
     for copy in started:
         copy.wait_send()
@@ -421,34 +378,28 @@
             vmem((2, 4, s_dev, 256), f32),
             vmem((2, 4, ny, 64, 256), bf16),
             vmem((2, 4, ny, 64, 256), bf16),
-            vmem((2, 3, ny, 64, 256), bf16),
-            vmem((2, 2, ny // 2, 64, 256), bf16),
-            vmem((2, 2, ny, 64, 256), bf16),
-            vmem((2, ny, 64, 256), f32),
-            vmem((2, ny - 1, 64, 256), bf16),
-            vmem((2, ny - 1, 64, 256), bf16),
+            vmem((2, NX, ny, 64, 256), bf16),
+            vmem((2, NX, ny, 64, 256), bf16),
             vmem((ny, 64, 512), bf16),
             vmem((128, 512), f32),
             vmem((n, 16, 512), f32),
-            vmem((nz, 4, 128), f32),
-            vmem((nz - 1, 4, 128), f32),
-            vmem((nz, 4, 128), f32),
-            vmem((NX, nz, 4, 128), f32),
-            vmem((ny, NC, NX, nz, 4, 128), f32),
+            vmem((4, 4, 512), f32),
+            vmem((3, 4, 512), f32),
+            vmem((nz // 4, 4, 512), f32),
+            vmem((4, 4, 512), f32),
+            vmem((NC, ny, NX, 4, 4, 512), f32),
             vmem((512, 512), f32),
             dma((2, 2, half, 2)), dma((2, 2, half, 2)),
             dma((6,)), dma((6,)),
             dma((2, 4)), dma((2, 4)),
-            dma((2, 2)), dma((2, 2)),
-            dma((2, 2, 2)), dma((2, 2, 2)),
-            dma((2, ny - 1)), dma((2, ny - 1)),
+            dma((2, NX, ny)), dma((2, NX, ny)),
             dma((2, ny - 1)), dma((2, ny - 1)),
             dma((n,)), dma((n,)),
-            dma((nz - 1,)), dma((nz - 1,)),
+            dma((3,)), dma((3,)),
             dma((ny,)), dma((ny,)),
-            dma((nz - 1,)), dma((nz - 1,)),
-            dma((NX - 1,)), dma((NX - 1,)),
-            dma((ny - 1,)), dma((ny - 1,)),
+            dma((nz // 4 - 1,)), dma((nz // 4 - 1,)),
+            dma((3,)), dma((3,)),
+            dma((NX, ny)), dma((NX, ny)),
         ],
         compiler_params=pltpu.CompilerParams(
             collective_id=0, has_side_effects=True, vmem_limit_bytes=58 << 20

time: 131 us -> 121 us (0.924)
  Pallas kernels: 129 us -> 120 us
    pallas_call x1, Pallas kernels: 129 us -> 120 us  [local(): pl.pallas_call(lambda *refs: kernel(nz, ny, s_dev * nz * NX, *refs), out_...]
where the time goes in v3:
time: 121 us
  Pallas kernels  120 us (99%)
  local copies, waits for them, and re-layouts  1.57 us (1%)
    pallas_call x1, Pallas kernels, local(): pl.pallas_call(lambda *refs: kernel(nz, ny, s_dev * nz * NX, *refs), out_...  120 us

profile of v3, /device:TPU:1, one launch (start us, length us, event | category | flops | bytes accessed | tf_op | source)
XLA Modules:
  0.0 121.3 jit_solution(6029468225530989652)
XLA Ops:
  0.0 119.7 %whiten.1 = f32[64,512]{1,0:T(8,128)} custom-call(bf16[2048,128]{1,0:T(8,128)(2,1)} %bitcast.5, s32[4,512]{1,0:T(4,128)} %bitcast.7, bf16[256,512]{1,0:T(8,128)(2,1)} %bitcast.6), custom_call_target="tpu_custom_call" | custom-call | tf_op jit(solution)/shard_map/whiten/pallas_call | solution.py:367
  119.7 1.6 %copy.5 = f32[64,512]{1,0:T(8,128)} copy(f32[64,512]{1,0:T(8,128)} %whiten.1) | data formatting | bytes 262144

commit v4 on v3

--- a/solution.py
+++ b/solution.py
@@ -46,11 +46,11 @@
 
 
 def kernel(
-    nz, ny, samples, grads, ids, probe, out,
-    ge, gx, codes, dense, pbuf, acc, csend, crecv, ps, pr,
+    nz, ny, samples, grads_in, ids_in, probe, out,
+    grads, ids, ge, gx, codes, dense, pbuf, acc, csend, crecv, ps, pr,
     sy, gram, gr, qs, qr, qall, ball, yall, whole,
     zss, zrs, xss, xrs, css, crs, pss, prs,
-    sss, srs, rss, rrs, ess, ers, fss, frs, ass, ars, bss, brs, dss, drs,
+    sss, srs, rss, rrs, ess, ers, fss, frs, ass, ars, bss, brs, dss, drs, ins,
 ):
     here = Place(nz, ny)
     z, x, y, c = here.z, here.x, here.y, here.c
@@ -66,8 +66,14 @@
     for other in near:
         pl.semaphore_signal(barrier, inc=1, device_id=other, device_id_type=MESH)
 
-    for h in range(2):
-        pbuf[h, 0] = probe[:, pl.ds(256 * h, 256)]
+    fetch = [pltpu.make_async_copy(grads_in, grads, ins.at[0]), pltpu.make_async_copy(ids_in, ids, ins.at[1])]
+    fetch += [
+        pltpu.make_async_copy(probe.at[:, pl.ds(256 * h, 256)], pbuf.at[h, 0], ins.at[2 + h]) for h in range(2)
+    ]
+    for copy in fetch:
+        copy.start()
+    for copy in fetch:
+        copy.wait()
     row = lax.broadcasted_iota(jnp.int32, (256, 256), 0)
     picked = 4 * lax.rem(row, 64) + row // 64 == lax.broadcasted_iota(jnp.int32, (256, 256), 1)
     pick = picked.astype(f32).astype(bf16)
@@ -269,9 +275,15 @@
             scopy(h, d).wait_recv()
     cx = [(dx, dc) for dx in range(NX) for dc in range(NC)][1:]
     cxdev = {p: here.at(dx=p[0], dc=p[1]) for p in cx}
-    right = sy[...].reshape(ny * 64, 512)
-    left = sy[:, :, pl.ds(pl.multiple_of(128 * y, 128), 128)].reshape(ny * 64, 128)
-    gram[...] = lax.dot_general(left, right, (((0,), (0,)), ((), ())), preferred_element_type=f32)
+    def block(r):
+        at = pl.multiple_of(128 * lax.rem(y + r, ny), 128)
+        return sy[:, :, pl.ds(at, 128)].reshape(ny * 64, 128)
+
+    left = block(0)
+    for r in range(3):
+        gram[:, pl.ds(128 * r, 128)] = lax.dot_general(
+            left, block(r), (((0,), (0,)), ((), ())), preferred_element_type=f32
+        )
     copies = []
     for n, (dx, dc) in enumerate(cx):
         at = 64 * lax.rem(c + dc, NC) + 16 * lax.rem(x + dx, NX)
@@ -336,7 +348,13 @@
             for xx in range(NX):
                 at = 128 * yy + 64 * cc + 16 * xx
                 for i in range(4):
-                    whole[at + 4 * i : at + 4 * i + 4, :] = yall[cc, yy, xx, i]
+                    rows = slice(at + 4 * i, at + 4 * i + 4)
+                    for r in range(3):
+                        to = 128 * ((yy + r) % ny)
+                        whole[rows, to : to + 128] = yall[cc, yy, xx, i, :, 128 * r : 128 * r + 128]
+    for yy in range(ny):
+        a, b = 128 * yy, 128 * ((yy + 3) % ny)
+        whole[a : a + 128, b : b + 128] = whole[b : b + 128, a : a + 128].T
     width = whole.shape[0]
     diag = lax.broadcasted_iota(jnp.int32, (width, width), 0) == lax.broadcasted_iota(jnp.int32, (width, width), 1)
     g = whole[...]
@@ -367,9 +385,11 @@
     return pl.pallas_call(
         lambda *refs: kernel(nz, ny, s_dev * nz * NX, *refs),
         out_shape=jax.ShapeDtypeStruct((64, 512), f32),
-        in_specs=[pl.BlockSpec(memory_space=pltpu.VMEM)] * 3,
+        in_specs=[pl.BlockSpec(memory_space=pl.ANY)] * 3,
         out_specs=pl.BlockSpec(memory_space=pltpu.VMEM),
         scratch_shapes=[
+            vmem((s_dev * 4, 128), bf16),
+            vmem((4, s_dev), jnp.int32),
             vmem((s_dev + 16, 512), bf16),
             vmem((3, s_dev + 16, 512), bf16),
             vmem((s_dev, 512), bf16),
@@ -381,13 +401,13 @@
             vmem((2, NX, ny, 64, 256), bf16),
             vmem((2, NX, ny, 64, 256), bf16),
             vmem((ny, 64, 512), bf16),
-            vmem((128, 512), f32),
-            vmem((n, 16, 512), f32),
-            vmem((4, 4, 512), f32),
-            vmem((3, 4, 512), f32),
-            vmem((nz // 4, 4, 512), f32),
-            vmem((4, 4, 512), f32),
-            vmem((NC, ny, NX, 4, 4, 512), f32),
+            vmem((128, 384), f32),
+            vmem((n, 16, 384), f32),
+            vmem((4, 4, 384), f32),
+            vmem((3, 4, 384), f32),
+            vmem((nz // 4, 4, 384), f32),
+            vmem((4, 4, 384), f32),
+            vmem((NC, ny, NX, 4, 4, 384), f32),
             vmem((512, 512), f32),
             dma((2, 2, half, 2)), dma((2, 2, half, 2)),
             dma((6,)), dma((6,)),
@@ -400,6 +420,7 @@
             dma((nz // 4 - 1,)), dma((nz // 4 - 1,)),
             dma((3,)), dma((3,)),
             dma((NX, ny)), dma((NX, ny)),
+            dma((4,)),
         ],
         compiler_params=pltpu.CompilerParams(
             collective_id=0, has_side_effects=True, vmem_limit_bytes=58 << 20

time: 121 us -> 119 us (0.983)
  Pallas kernels: 120 us -> 117 us
    pallas_call x1, Pallas kernels: 120 us -> 117 us  [local(): pl.pallas_call(lambda *refs: kernel(nz, ny, s_dev * nz * NX, *refs), out_...]
where the time goes in v4:
time: 119 us
  Pallas kernels  117 us (98%)
  local copies, waits for them, and re-layouts  1.57 us (1%)
    pallas_call x1, Pallas kernels, local(): pl.pallas_call(lambda *refs: kernel(nz, ny, s_dev * nz * NX, *refs), out_...  117 us

profile of v4, /device:TPU:1, one launch (start us, length us, event | category | flops | bytes accessed | tf_op | source)
XLA Modules:
  0.0 119.0 jit_solution(17816085018513265081)
XLA Ops:
  0.0 117.4 %whiten.1 = f32[64,512]{1,0:T(8,128)} custom-call(bf16[2048,128]{1,0:T(8,128)(2,1)} %bitcast.5, s32[4,512]{1,0:T(4,128)} %bitcast.7, bf16[256,512]{1,0:T(8,128)(2,1)} %bitcast.6), custom_call_target="tpu_custom_call" | custom-call | tf_op jit(solution)/shard_map/whiten/pallas_call | solution.py:385
  117.4 1.6 %copy.5 = f32[64,512]{1,0:T(8,128)} copy(f32[64,512]{1,0:T(8,128)} %whiten.1) | data formatting | bytes 262144

commit v5 on v4

--- a/solution.py
+++ b/solution.py
@@ -217,7 +217,7 @@
         go(xc["fb"])
 
     def last(h, t):
-        product(h, t, late, False)
+        product(h, t, end if h else late, False)
         give_core(h, t)
 
     def first(h, t):
@@ -229,6 +229,7 @@
 
     lag = 2
     early, late = [(0, 6), (11, nz)], [(6, 11)]
+    mid, end = [(6, 8), (9, 11)], [(8, 9)]
     work = {
         1: [pass_a, pass_b],
         3: [
@@ -252,6 +253,9 @@
                 go(xc[name])
             expand(0, 0)
             expand(0, 1)
+        if e == half + lag - 1:
+            for t in (3, 2, 1, 0):
+                product(1, t, mid, False)
         for w in range(2):
             for h in parts:
                 arrive(h, e - lag * h, w)

time: 119 us -> 119 us (level)
  no operation moved by 1% of the time
where the time goes in v5:
time: 119 us
  Pallas kernels  117 us (98%)
  local copies, waits for them, and re-layouts  1.57 us (1%)
    pallas_call x1, Pallas kernels, local(): pl.pallas_call(lambda *refs: kernel(nz, ny, s_dev * nz * NX, *refs), out_...  117 us

profile of v5, /device:TPU:1, one launch (start us, length us, event | category | flops | bytes accessed | tf_op | source)
XLA Modules:
  0.0 118.8 jit_solution(8891300589154561421)
XLA Ops:
  0.0 117.3 %whiten.1 = f32[64,512]{1,0:T(8,128)} custom-call(bf16[2048,128]{1,0:T(8,128)(2,1)} %bitcast.5, s32[4,512]{1,0:T(4,128)} %bitcast.7, bf16[256,512]{1,0:T(8,128)(2,1)} %bitcast.6), custom_call_target="tpu_custom_call" | custom-call | tf_op jit(solution)/shard_map/whiten/pallas_call | solution.py:389
  117.3 1.6 %copy.5 = f32[64,512]{1,0:T(8,128)} copy(f32[64,512]{1,0:T(8,128)} %whiten.1) | data formatting | bytes 262144
